TPU v7x, 32 devices: a whole 2x2x4 slice. The times are simulated.
32 devices in a mesh: grid: 8 (over y, x, core), ipts: 4 (over z).
Axes of the slice: x: 2, y: 2, z: 4, core: 2. Of those that a mesh axis runs over, the one named last changes fastest.
Arguments:
- orbitals: bfloat16 [16384, 1024], P(('grid', 'ipts')), may hold values from -1.1953125 to 1.1953125
- targets: bfloat16 [16384, 256], P(('grid', 'ipts')), may hold values from -6 to 6
- points: int32 [4, 1024], P('ipts', 'grid'), may hold values from 0 to 16383, as said below
- potential: bfloat16 [16384, 4096], P('grid', 'ipts'), may hold values from -0.09375 to 0.09375
Outputs:
- exchanged: bfloat16 [16384, 256], P(('grid', 'ipts'))
Inputs may be any that keep to these rules, and one draw needn't show every extreme that they name: Indices are distinct over all groups; each row of points rises strictly, and its entries k * 128 to (k + 1) * 128 - 1 lie in grid rows k * 2048 to (k + 1) * 2048 - 1.
All inputs are finite; a program needn't handle non-finite values.
Results may differ from a plain program's by a relative error of at most 0.0049.
Values may be sent and summed in bfloat16 or wider, within the bound.
A program may use at most 128 MiB of HBM per device.

v0:
```python
import jax
import jax.numpy as jnp
from jax import lax
from jax.sharding import PartitionSpec as P


def local(orbitals, targets, points, potential):
    groups = lax.axis_size("ipts")
    own_rows = orbitals.shape[0]
    slab_length = own_rows * groups
    slab_start = lax.axis_index("grid") * slab_length
    whole_slab = lax.all_gather(orbitals, "ipts", axis=0, tiled=True)
    every_group = lax.all_gather(points, "ipts", axis=0, tiled=True)
    orbital_values = jnp.take(whole_slab, points[0] - slab_start, axis=0)
    offset = every_group - (slab_start + lax.axis_index("ipts") * own_rows)
    inside = (offset >= 0) & (offset < own_rows)
    clipped = jnp.clip(offset, 0, own_rows - 1)
    picked = jnp.take(targets, clipped, axis=0) * inside[:, :, None].astype(targets.dtype)
    summed = lax.psum_scatter(picked, "ipts", scatter_dimension=0, tiled=True).astype(jnp.float32)
    target_values = summed[0].astype(jnp.bfloat16)
    orbital_piece = lax.all_gather(orbital_values, "grid", axis=0, tiled=True)
    target_piece = lax.all_gather(target_values, "grid", axis=0, tiled=True)
    products = lax.dot_general(
        whole_slab, orbital_piece, (((1,), (1,)), ((), ())), preferred_element_type=jnp.float32
    )
    weighted = (potential * products).astype(jnp.bfloat16)
    group_total = jnp.dot(weighted, target_piece, preferred_element_type=jnp.float32)
    summed_rows = lax.psum_scatter(group_total, "ipts", scatter_dimension=0, tiled=True)
    return (-summed_rows).astype(jnp.bfloat16)


def solution(mesh):
    placed = (
        P(("grid", "ipts"), None),
        P(("grid", "ipts"), None),
        P("ipts", "grid"),
        P("grid", "ipts"),
    )
    return jax.shard_map(
        local, mesh=mesh, in_specs=placed, out_specs=P(("grid", "ipts"), None), check_vma=False
    )
```

profile of v0, /device:TPU:0, one launch (start us, length us, event | category | flops | bytes accessed | tf_op | source)
XLA Modules:
  0.0 204.3 jit_solution(11490571779918535644)
XLA Ops:
  6.5 0.0 copy-start
  6.5 0.0 copy-start.1
  6.5 0.0 all-gather.5.cloned.1.call-start
  6.5 0.7 all-gather.5.cloned.1.call-update
  7.3 0.0 reduce-scatter.3.cloned.1.call-start
  7.3 12.8 %all-gather.1 = s32[4,1,128]{2,1,0:T(1,128)S(1)} all-gather(s32[1,1,128]{2,1,0:T(1,128)} %bitcast.29), channel_id=1, replica_groups=mesh['grid'=8,'ipts'=4] {'ipts'}, dimensions={0}, use_global_device_ids=true | all-gather | bytes 2560 | tf_op jit(solution)/shard_map/all_gather | solution.py:13
  20.2 0.0 copy-done
  20.2 2.0 gather_fusion.1
  22.2 0.9 select_multiply_fusion
  23.1 0.0 reduce-scatter.3.cloned.1.call-update
  23.1 0.0 all-gather.7.cloned.1.call-start
  23.2 0.0 copy-done.1
  23.2 69.2 %all-gather.5.cloned.1.call-done = bf16[2048,1024]{1,0:T(8,128)(2,1)} async-done(((bf16[512,1024]{1,0:T(8,128)(2,1)}), bf16[2048,1024]{1,0:T(8,128)(2,1)}) %all-gather.5.cloned.1.call-update) | async-done | bytes 4194320 | tf_op jit(solution)/shard_map/all_gather | solution.py:12
  92.4 3.8 %gather_fusion = bf16[128,1024]{1,0:T(8,128)(2,1)S(1)} fusion(bf16[2048,1024]{1,0:T(8,128)(2,1)} %all-gather.5.cloned.1.call-done, s32[1024]{0:T(1024)S(1)} %pad_clamp_fusion.1), kind=kCustom, calls=%fused_computation | custom fusion | bytes 524800 | tf_op jit(solution)/shard_map/jit(_take)/gather | solution.py:14
  96.2 0.8 broadcast_select_fusion
  97.0 0.0 all-gather.7.cloned.1.call-update
  97.0 0.0 reduce-scatter.5.cloned.1.call-start
  97.0 6.5 %copy.5 = bf16[2048,1024]{0,1:T(8,128)(2,1)} copy(bf16[2048,1024]{1,0:T(8,128)(2,1)} %param.7) | data formatting | bytes 8388608 | tf_op args[3]
  103.6 9.6 %reduce-scatter.3.cloned.1.call-done = bf16[1,128,256]{2,1,0:T(8,128)(2,1)} async-done(((bf16[4,128,256]{2,1,0:T(8,128)(2,1)}), bf16[1,128,256]{2,1,0:T(8,128)(2,1)}) %reduce-scatter.3.cloned.1.call-update) | async-done | bytes 65552 | tf_op jit(solution)/shard_map/reduce_scatter | solution.py:19
  113.2 10.1 %all-gather = bf16[1,1024,256]{2,1,0:T(8,128)(2,1)S(1)} all-gather(bf16[1,128,256]{2,1,0:T(8,128)(2,1)} %reduce-scatter.3.cloned.1.call-done), channel_id=2, replica_groups=mesh['grid'=8,'ipts'=4] {'grid'}, dimensions={1}, use_global_device_ids=true | all-gather | bytes 589824 | tf_op jit(solution)/shard_map/all_gather | solution.py:22
  123.3 17.8 %all-gather.7.cloned.1.call-done = bf16[1024,1024]{1,0:T(8,128)(2,1)} async-done(((bf16[128,1024]{1,0:T(8,128)(2,1)}), bf16[1024,1024]{1,0:T(8,128)(2,1)}) %all-gather.7.cloned.1.call-update) | async-done | bytes 2097168 | tf_op jit(solution)/shard_map/all_gather | solution.py:21
  141.1 11.0 %fusion.1 = f32[2048,256]{1,0:T(8,128)} fusion(bf16[2048,1024]{0,1:T(8,128)(2,1)} %copy.5, bf16[1024,1024]{1,0:T(8,128)(2,1)} %all-gather.7.cloned.1.call-done, bf16[2048,1024]{1,0:T(8,128)(2,1)} %all-gather.5.cloned.1.call-done, bf16[1,1024,256]{2,1,0:T(8,128)(2,1)S(1)} %all-gather), kind=kOutput, calls=%fused_computation.4 | convolution fusion | flops 5375000576 | bytes 13107200 | tf_op jit(solution)/shard_map/dot_general | solution.py:27
  152.1 0.0 reduce-scatter.5.cloned.1.call-update
  152.2 43.8 %reduce-scatter.5.cloned.1.call-done = f32[512,256]{1,0:T(8,128)} async-done(((f32[2048,256]{1,0:T(8,128)}), f32[512,256]{1,0:T(8,128)}) %reduce-scatter.5.cloned.1.call-update) | async-done | bytes 524304 | tf_op jit(solution)/shard_map/reduce_scatter | solution.py:28
  195.9 1.8 negate_convert_fusion
  (9 shorter events, 0.1 us)
Async XLA Ops:
  6.5 13.6 %copy-start = (bf16[512,256]{1,0:T(8,128)(2,1)S(1)}, bf16[512,256]{1,0:T(8,128)(2,1)}, u32[]{:S(2)}) copy-start(bf16[512,256]{1,0:T(8,128)(2,1)} %param.5) | copy-start | bytes 786436
  6.5 16.6 %copy-start.1 = (s32[1,128]{1,0:T(1,128)S(1)}, s32[1,128]{1,0:T(1,128)}, u32[]{:S(2)}) copy-start(s32[1,128]{1,0:T(1,128)} %param.6) | copy-start | bytes 1540
  6.5 85.9 %all-gather.5.cloned.1.call-start = ((), (), s32[]{:S(2)}) async-start(), calls=%async_computation.2 | async-start | bytes 5242880 | tf_op jit(solution)/shard_map/all_gather | solution.py:12
  7.3 105.9 %reduce-scatter.3.cloned.1.call-start = ((), (), s32[]{:S(2)}) async-start(), calls=%async_computation.4 | async-start | bytes 327680 | tf_op jit(solution)/shard_map/reduce_scatter | solution.py:19
  23.1 118.0 %all-gather.7.cloned.1.call-start = ((), (), s32[]{:S(2)}) async-start(), calls=%async_computation.3 | async-start | bytes 2359296 | tf_op jit(solution)/shard_map/all_gather | solution.py:21
  97.0 98.9 %reduce-scatter.5.cloned.1.call-start = ((), (), s32[]{:S(2)}) async-start(), calls=%async_computation.5 | async-start | bytes 2621440 | tf_op jit(solution)/shard_map/reduce_scatter | solution.py:28
Sparse Core Ops, SparseCore 0:
  8.9 83.4 all-gather.4
  94.7 18.4 reduce-scatter.2
  115.1 25.9 all-gather.6
  152.3 43.6 reduce-scatter.4
where the time goes:
time: 205 us; the launch traced here: 204 us
  waiting for transfers between devices  141 us (69%)
  blocking collectives  22.9 us (11%)
  between operations  13.2 us (6%)
  local copies, waits for them, and re-layouts  12.3 us (6%)
  matrix products  11 us (5%)
  other arithmetic  3.55 us (2%)
    all_gather x1, waiting for transfers between devices, local(): whole_slab = lax.all_gather(orbitals, 'ipts', axis=0, tiled=True)  69.2 us
    reduce_scatter x1, waiting for transfers between devices, local(): lax.psum_scatter(group_total, 'ipts', scatter_dimension=0, tiled=True)  43.8 us
    all_gather x1, waiting for transfers between devices, local(): orbital_piece = lax.all_gather(orbital_values, 'grid', axis=0, tiled=True)  17.8 us
    all_gather x1, blocking collectives, local(): every_group = lax.all_gather(points, 'ipts', axis=0, tiled=True)  12.8 us
    dot_general x1, matrix products, local(): jnp.dot(weighted, target_piece, preferred_element_type=jnp.float32)  11 us
    all_gather x1, blocking collectives, local(): target_piece = lax.all_gather(target_values, 'grid', axis=0, tiled=True)  10.1 us
    reduce_scatter x1, waiting for transfers between devices, local(): lax.psum_scatter(picked, 'ipts', scatter_dimension=0, tiled=True)  9.59 us
    unnamed x6, local copies, waits for them, and re-layouts  6.53 us
  transfers between devices with their start and end apart: 4, of which 4 were waited for; matrix products, arithmetic and copies ran while one was open for 7% of the time, Pallas kernels for 0%

commit v1 on v0

--- a/solution.py
+++ b/solution.py
@@ -9,7 +9,14 @@
     own_rows = orbitals.shape[0]
     slab_length = own_rows * groups
     slab_start = lax.axis_index("grid") * slab_length
-    whole_slab = lax.all_gather(orbitals, "ipts", axis=0, tiled=True)
+    size = lax.axis_size("ipts")
+    right = [(i, (i + 1) % size) for i in range(size)]
+    parts = [orbitals]
+    for reach in range(1, size):
+        parts = [lax.ppermute(parts[0], "ipts", right), *parts]
+    whole = jnp.concatenate(parts, axis=0)
+    shift = (lax.axis_index("ipts") + 1) * parts[-1].shape[0]
+    whole_slab = jnp.roll(whole, shift, axis=0)
     every_group = lax.all_gather(points, "ipts", axis=0, tiled=True)
     orbital_values = jnp.take(whole_slab, points[0] - slab_start, axis=0)
     offset = every_group - (slab_start + lax.axis_index("ipts") * own_rows)

time: 205 us -> 193 us (0.941)
  waiting for transfers between devices: 141 us -> 105 us
  blocking collectives: 22.9 us -> 39 us
  starting transfers between devices: 0.12 us -> 5.03 us
  other arithmetic: 3.55 us -> 5.79 us
    all_gather x1 -> x0, waiting for transfers between devices: 69.2 us -> none  [local(): whole_slab = lax.all_gather(orbitals, 'ipts', axis=0, tiled=True)]
    ppermute x0 -> x3, waiting for transfers between devices: none -> 46.7 us  [local(): parts = [lax.ppermute(parts[0], 'ipts', right), *parts]]
    all_gather x1, blocking collectives: 12.8 us -> 28 us  [local(): every_group = lax.all_gather(points, 'ipts', axis=0, tiled=True)]
    reduce_scatter x1, waiting for transfers between devices: 9.59 us -> 0.02 us  [local(): lax.psum_scatter(picked, 'ipts', scatter_dimension=0, tiled=True)]
    ppermute x0 -> x3, starting transfers between devices: none -> 4.94 us  [local(): parts = [lax.ppermute(parts[0], 'ipts', right), *parts]]
    unnamed x6 -> x12, local copies, waits for them, and re-layouts: 6.53 us -> 2.95 us
    all_gather x1, waiting for transfers between devices: 17.8 us -> 14.5 us  [local(): orbital_piece = lax.all_gather(orbital_values, 'grid', axis=0, tiled=True)]
    dynamic_slice x0 -> x1, local copies, waits for them, and re-layouts: none -> 2.38 us  [local(): whole_slab = jnp.roll(whole, shift, axis=0)]
  transfers between devices with their start and end apart: 4 -> 6, of which waited for: 4 -> 4; matrix products, arithmetic and copies ran while one was open for 7% -> 8% of each run, Pallas kernels for 0% -> 0%
where the time goes in v1:
time: 193 us
  waiting for transfers between devices  105 us (54%)
  blocking collectives  39 us (20%)
  between operations  15 us (8%)
  local copies, waits for them, and re-layouts  11.8 us (6%)
  matrix products  11.2 us (6%)
  other arithmetic  5.79 us (3%)
  starting transfers between devices  5.03 us (3%)
    ppermute x3, waiting for transfers between devices, local(): parts = [lax.ppermute(parts[0], 'ipts', right), *parts]  46.7 us
    reduce_scatter x1, waiting for transfers between devices, local(): lax.psum_scatter(group_total, 'ipts', scatter_dimension=0, tiled=True)  43.8 us
    all_gather x1, blocking collectives, local(): every_group = lax.all_gather(points, 'ipts', axis=0, tiled=True)  28 us
    all_gather x1, waiting for transfers between devices, local(): orbital_piece = lax.all_gather(orbital_values, 'grid', axis=0, tiled=True)  14.5 us
    dot_general x1, matrix products, local(): jnp.dot(weighted, target_piece, preferred_element_type=jnp.float32)  11.2 us
    all_gather x1, blocking collectives, local(): target_piece = lax.all_gather(target_values, 'grid', axis=0, tiled=True)  11.1 us
    ppermute x3, starting transfers between devices, local(): parts = [lax.ppermute(parts[0], 'ipts', right), *parts]  4.94 us
  transfers between devices with their start and end apart: 6, of which 4 were waited for; matrix products, arithmetic and copies ran while one was open for 8% of the time, Pallas kernels for 0%

profile of v1, /device:TPU:0, one launch (start us, length us, event | category | flops | bytes accessed | tf_op | source)
XLA Modules:
  0.0 192.8 jit_solution(12178539948833164961)
XLA Ops:
  7.4 0.0 copy-start
  7.4 0.0 copy-start.1
  7.4 0.0 reduce-scatter.3.cloned.1.call-start
  7.4 3.1 %collective-permute-start = (bf16[512,1024]{1,0:T(8,128)(2,1)}, bf16[512,1024]{1,0:T(8,128)(2,1)S(1)}, u32[]{:S(2)}, u32[]{:S(2)}) collective-permute-start(bf16[512,1024]{1,0:T(8,128)(2,1)} %param.4), channel_id=1, source_target_pairs={{0,1},{1,2},{2,3},{3,0},{4,5},{5,6},{6,7},{7,4},{8,9},{9,10},{10,1... | collective-permute-start | bytes 3145736 | tf_op jit(solution)/shard_map/ppermute | solution.py:16
  10.4 25.4 %collective-permute-done = bf16[512,1024]{1,0:T(8,128)(2,1)S(1)} collective-permute-done((bf16[512,1024]{1,0:T(8,128)(2,1)}, bf16[512,1024]{1,0:T(8,128)(2,1)S(1)}, u32[]{:S(2)}, u32[]{:S(2)}) %collective-permute-start) | collective-permute-done | bytes 1048608 | tf_op jit(solution)/shard_map/ppermute | solution.py:16
  35.8 0.0 collective-permute-start.1
  35.9 28.0 %all-gather.1 = s32[4,1,128]{2,1,0:T(1,128)S(1)} all-gather(s32[1,1,128]{2,1,0:T(1,128)} %bitcast.23), channel_id=1, replica_groups=mesh['grid'=8,'ipts'=4] {'ipts'}, dimensions={0}, use_global_device_ids=true | all-gather | bytes 2560 | tf_op jit(solution)/shard_map/all_gather | solution.py:20
  63.8 0.0 collective-permute-done.1
  63.9 1.9 collective-permute-start.2
  65.8 0.0 copy-done
  65.8 2.6 %gather_fusion.1 = bf16[512,256]{1,0:T(8,128)(2,1)} fusion(bf16[512,256]{1,0:T(8,128)(2,1)S(1)} %copy-done, s32[1024]{0:T(1024)S(1)} %pad_clamp_fusion), kind=kCustom, calls=%fused_computation.1 | custom fusion | bytes 526336 | tf_op jit(solution)/shard_map/jit(_take)/gather | solution.py:25
  68.4 1.9 select_multiply_fusion
  70.2 0.0 reduce-scatter.3.cloned.1.call-update
  70.2 0.0 all-gather.4.cloned.1.call-start
  70.3 0.7 fusion.3
  71.0 0.7 compare_and_fusion.1
  71.6 21.3 %collective-permute-done.2 = bf16[512,1024]{1,0:T(8,128)(2,1)} collective-permute-done((bf16[512,1024]{1,0:T(8,128)(2,1)S(1)}, bf16[512,1024]{1,0:T(8,128)(2,1)}, u32[]{:S(2)}, u32[]{:S(2)}) %collective-permute-start.2) | collective-permute-done | bytes 1048608 | tf_op jit(solution)/shard_map/ppermute | solution.py:16
  92.9 1.3 constant_dynamic-update-slice_fusion.7
  94.2 0.1 constant_dynamic-update-slice_fusion.6
  94.3 0.1 constant_dynamic-update-slice_fusion.5
  94.4 0.0 copy-done.1
  94.4 0.1 constant_dynamic-update-slice_fusion.4
  94.5 1.3 constant_dynamic-update-slice_fusion.3
  95.8 0.1 constant_dynamic-update-slice_fusion.2
  95.8 0.1 constant_dynamic-update-slice_fusion.1
  95.9 0.1 constant_dynamic-update-slice_fusion
  96.0 2.4 %constant_dynamic-slice_fusion = bf16[2048,1024]{1,0:T(8,128)(2,1)} fusion(bf16[4096,1024]{1,0:T(8,128)(2,1)S(1)} %constant_dynamic-update-slice_fusion, s32[]{:T(128)S(6)} %select_n.43), kind=kLoop, calls=%fused_computation.28 | loop fusion | bytes 8388612 | tf_op jit(solution)/shard_map/jit(_roll_dynamic)/dynamic_slice | solution.py:19
  98.4 3.8 %gather_fusion = bf16[128,1024]{1,0:T(8,128)(2,1)S(1)} fusion(bf16[2048,1024]{1,0:T(8,128)(2,1)} %constant_dynamic-slice_fusion, s32[1024]{0:T(1024)S(1)} %pad_clamp_fusion.1), kind=kCustom, calls=%fused_computation | custom fusion | bytes 524800 | tf_op jit(solution)/shard_map/jit(_take)/gather | solution.py:21
  102.1 0.8 broadcast_select_fusion
  102.9 0.0 all-gather.4.cloned.1.call-update
  103.0 0.0 reduce-scatter.5.cloned.1.call-start
  103.0 0.0 reduce-scatter.3.cloned.1.call-done
  103.0 11.1 %all-gather = bf16[1,1024,256]{2,1,0:T(8,128)(2,1)S(1)} all-gather(bf16[1,128,256]{2,1,0:T(8,128)(2,1)} %reduce-scatter.3.cloned.1.call-done), channel_id=2, replica_groups=mesh['grid'=8,'ipts'=4] {'grid'}, dimensions={1}, use_global_device_ids=true | all-gather | bytes 589824 | tf_op jit(solution)/shard_map/all_gather | solution.py:29
  114.1 14.5 %all-gather.4.cloned.1.call-done = bf16[1024,1024]{1,0:T(8,128)(2,1)} async-done(((bf16[128,1024]{1,0:T(8,128)(2,1)}), bf16[1024,1024]{1,0:T(8,128)(2,1)}) %all-gather.4.cloned.1.call-update) | async-done | bytes 2097168 | tf_op jit(solution)/shard_map/all_gather | solution.py:28
  128.6 11.2 %fusion = f32[2048,256]{1,0:T(8,128)} fusion(bf16[2048,1024]{1,0:T(8,128)(2,1)} %param.7, bf16[2048,1024]{1,0:T(8,128)(2,1)} %constant_dynamic-slice_fusion, bf16[1024,1024]{1,0:T(8,128)(2,1)} %all-gather.4.cloned.1.call-done, bf16[1,1024,256]{2,1,0:T(8,128)(2,1)S(1)} %all-gather), kind=kOutput, calls=%fused_computation.3 | convolution fusion | flops 5375000576 | bytes 13107200 | tf_op jit(solution)/shard_map/dot_general | solution.py:34
  139.7 0.0 reduce-scatter.5.cloned.1.call-update
  139.8 43.8 %reduce-scatter.5.cloned.1.call-done = f32[512,256]{1,0:T(8,128)} async-done(((f32[2048,256]{1,0:T(8,128)}), f32[512,256]{1,0:T(8,128)}) %reduce-scatter.5.cloned.1.call-update) | async-done | bytes 524304 | tf_op jit(solution)/shard_map/reduce_scatter | solution.py:35
  183.6 1.8 negate_convert_fusion
  (7 shorter events, 0.0 us)
Async XLA Ops:
  7.4 58.4 %copy-start = (bf16[512,256]{1,0:T(8,128)(2,1)S(1)}, bf16[512,256]{1,0:T(8,128)(2,1)}, u32[]{:S(2)}) copy-start(bf16[512,256]{1,0:T(8,128)(2,1)} %param.5) | copy-start | bytes 786436
  7.4 87.0 %copy-start.1 = (bf16[512,1024]{1,0:T(8,128)(2,1)S(1)}, bf16[512,1024]{1,0:T(8,128)(2,1)}, u32[]{:S(2)}) copy-start(bf16[512,1024]{1,0:T(8,128)(2,1)} %param.4) | copy-start | bytes 3145732
  7.4 95.7 %reduce-scatter.3.cloned.1.call-start = ((), (), s32[]{:S(2)}) async-start(), calls=%async_computation.3 | async-start | bytes 327680 | tf_op jit(solution)/shard_map/reduce_scatter | solution.py:26
  7.4 28.5 %collective-permute-start = (bf16[512,1024]{1,0:T(8,128)(2,1)}, bf16[512,1024]{1,0:T(8,128)(2,1)S(1)}, u32[]{:S(2)}, u32[]{:S(2)}) collective-permute-start(bf16[512,1024]{1,0:T(8,128)(2,1)} %param.4), channel_id=1, source_target_pairs={{0,1},{1,2},{2,3},{3,0},{4,5},{5,6},{6,7},{7,4},{8,9},{9,10},{10,1... | collective-permute-start | bytes 3145736 | tf_op jit(solution)/shard_map/ppermute | solution.py:16
  35.8 28.0 %collective-permute-start.1 = (bf16[512,1024]{1,0:T(8,128)(2,1)S(1)}, bf16[512,1024]{1,0:T(8,128)(2,1)S(1)}, u32[]{:S(2)}, u32[]{:S(2)}) collective-permute-start(bf16[512,1024]{1,0:T(8,128)(2,1)S(1)} %collective-permute-done), channel_id=1, source_target_pairs={{0,1},{1,2},{2,3},{3,0},{4,5},{5,6},{6,7},{7,4},{8,9},{9,10},{10,1... | collective-permute-start | bytes 3145736 | tf_op jit(solution)/shard_map/ppermute | solution.py:16
  63.9 29.1 %collective-permute-start.2 = (bf16[512,1024]{1,0:T(8,128)(2,1)S(1)}, bf16[512,1024]{1,0:T(8,128)(2,1)}, u32[]{:S(2)}, u32[]{:S(2)}) collective-permute-start(bf16[512,1024]{1,0:T(8,128)(2,1)S(1)} %collective-permute-done.1), channel_id=1, source_target_pairs={{0,1},{1,2},{2,3},{3,0},{4,5},{5,6},{6,7},{7,4},{8,9},{9,10},{10,1... | collective-permute-start | bytes 3145736 | tf_op jit(solution)/shard_map/ppermute | solution.py:16
  70.2 58.3 %all-gather.4.cloned.1.call-start = ((), (), s32[]{:S(2)}) async-start(), calls=%async_computation.2 | async-start | bytes 2359296 | tf_op jit(solution)/shard_map/all_gather | solution.py:28
  103.0 80.6 %reduce-scatter.5.cloned.1.call-start = ((), (), s32[]{:S(2)}) async-start(), calls=%async_computation.4 | async-start | bytes 2621440 | tf_op jit(solution)/shard_map/reduce_scatter | solution.py:35
Sparse Core Ops, SparseCore 0:
  70.4 21.4 reduce-scatter.2
  139.9 43.6 reduce-scatter.4
Sparse Core Ops, SparseCore 1:
  103.1 25.5 all-gather.3
